TPU v7x, 256 devices: a whole 4x4x8 slice. The times are simulated.
256 devices in a mesh: rows: 16 (over z, x_hi), vocab: 16 (over x_lo, y, core).
Axes of the slice: x: 4 (x_hi: 2, x_lo: 2; x = x_hi * 2 + x_lo), y: 4, z: 8, core: 2. Of those that a mesh axis runs over, the one named last changes fastest.
Arguments:
- hidden_rows: bfloat16 [512, 8192], P('vocab', 'rows'), may hold values from -24 to 24
- row_states: int32 [512], P('vocab'), may hold values from 0 to 511
- head_weight: bfloat16 [8192, 152064], P(None, ('rows', 'vocab')), may hold values from -2 to 2
- grammar_table: int32 [512, 152064], P(None, ('rows', 'vocab')), may hold values from 0 to 1, as said below
Outputs:
- log_probs: float32 [512, 152064], P(None, ('rows', 'vocab'))
- normalizer: float32 [512], replicated
Inputs may be any that keep to these rules, and one draw needn't show every extreme that they name: `grammar_table`: every state allows the tokens 0 to 31.
All inputs are finite; a program needn't handle non-finite values.
Results may differ from a plain program's by a relative error of at most 0.0003.
Values may be sent and summed in bfloat16 or wider, within the bound.
A program may use at most 64 MiB of HBM per device.

v0:
```python
import jax
import jax.numpy as jnp
from jax import lax
from jax.sharding import PartitionSpec as P

lowest = -1e30


def passed_along(block, axis, distance):
    devices = range(lax.axis_size(axis))
    route = [((i - distance) % len(devices), i) for i in devices]
    return lax.ppermute(block, axis, route)


def stop_parts(row_block, state_marks, head_weight, table_mask):
    logits = jnp.dot(row_block, head_weight, preferred_element_type=jnp.float32)
    allowed = jnp.dot(state_marks, table_mask, preferred_element_type=jnp.float32)
    keep_mask = allowed > 0.5
    row_peak = jnp.max(jnp.where(keep_mask, logits, lowest), axis=1)
    exp_total = jnp.sum(jnp.where(keep_mask, jnp.exp(logits - row_peak[:, None]), 0.0), axis=1)
    return (logits, allowed.astype(jnp.bfloat16), row_peak, exp_total)


def local(hidden_rows, row_states, head_weight, grammar_table):
    rows_blk = hidden_rows.shape[0]
    vocab_count = lax.axis_size("vocab")
    state_count = grammar_table.shape[0]
    columns = head_weight.shape[1]
    all_rows = rows_blk * vocab_count
    row_block = lax.all_gather(hidden_rows, "rows", axis=1, tiled=True)
    onehot = (row_states[:, None] == jnp.arange(state_count, dtype=jnp.int32)[None, :]).astype(
        jnp.bfloat16
    )
    table_mask = grammar_table.astype(jnp.bfloat16)
    buffers = (
        jnp.zeros((all_rows, columns), jnp.float32),
        jnp.zeros((all_rows, columns), jnp.bfloat16),
        jnp.full((all_rows,), lowest, jnp.float32),
        jnp.zeros((all_rows,), jnp.float32),
    )

    def record(stores, pieces, row_start):
        logits, allowed, row_peak, exp_total = stop_parts(
            pieces[0], pieces[1], head_weight, table_mask
        )
        logit_buf, allow_buf, peak_buf, total_buf = stores
        logit_buf = lax.dynamic_update_slice_in_dim(logit_buf, logits, row_start, 0)
        allow_buf = lax.dynamic_update_slice_in_dim(allow_buf, allowed, row_start, 0)
        peak_buf = lax.dynamic_update_slice_in_dim(peak_buf, row_peak, row_start, 0)
        total_buf = lax.dynamic_update_slice_in_dim(total_buf, exp_total, row_start, 0)
        return (logit_buf, allow_buf, peak_buf, total_buf)

    own_index = lax.axis_index("vocab")
    buffers = record(buffers, (row_block, onehot), own_index * rows_blk)

    def advance(section_num, carry):
        moving, moving_marks, stores = carry
        moving, moving_marks = passed_along((moving, moving_marks), "vocab", 1)
        anchor = jnp.mod(own_index - section_num, vocab_count)
        stores = record(stores, (moving, moving_marks), anchor * rows_blk)
        return (moving, moving_marks, stores)

    _, _, buffers = lax.fori_loop(1, vocab_count, advance, (row_block, onehot, buffers))
    logit_buf, allow_buf, peak_buf, total_buf = buffers
    row_peak = lax.pmax(peak_buf, ("rows", "vocab"))
    exp_total = lax.psum(total_buf * jnp.exp(peak_buf - row_peak), ("rows", "vocab"))
    normalizer = row_peak + jnp.log(exp_total)
    log_probs = jnp.where(allow_buf > 0.5, logit_buf - normalizer[:, None], 0.0)
    return (log_probs, normalizer)


def solution(mesh):
    placed = (
        P("vocab", "rows"),
        P("vocab"),
        P(None, ("rows", "vocab")),
        P(None, ("rows", "vocab")),
    )
    return jax.shard_map(
        local,
        mesh=mesh,
        in_specs=placed,
        out_specs=(P(None, ("rows", "vocab")), P()),
        check_vma=False,
    )
```

profile of v0, /device:TPU:1, one launch (start us, length us, event | category | flops | bytes accessed | tf_op | source)
XLA Modules:
  0.0 513.2 jit_solution(8244974761511444929)
XLA Ops:
  1.4 43.1 %all_gather.3 = bf16[32,8192]{1,0:T(8,128)(2,1)} all-gather(bf16[32,512]{1,0:T(8,128)(2,1)} %param.6), channel_id=1, replica_groups=mesh['rows'=16,'vocab'=16] {'rows'}, dimensions={1}, use_global_device_ids=true | all-gather | bytes 557056 | tf_op jit(solution)/shard_map/all_gather | solution.py:30
  47.1 7.0 %select_reduce_fusion.3 = (f32[32]{0:T(128)S(1)}, pred[32,594]{1,0:T(8,128)(4,1)S(1)}, f32[32,594]{1,0:T(8,128)S(1)}) fusion(f32[32,594]{1,0:T(8,128)S(1)} %get-tuple-element.292, bf16[32,8192]{1,0:T(8,128)(2,1)} %all_gather.3, bf16[8192,594]{0,1:T(8,128)(2,1)} %param.8), kind=kOutput, calls=%fused_computation.7 | convolution fusion | flops 311484064 | bytes 10427584 | tf_op jit(solution)/shard_map/dot_general | solution.py:16
  61.4 294.7 %while.25 = (s32[]{:T(128)}, bf16[32,8192]{1,0:T(8,128)(2,1)}, bf16[32,512]{1,0:T(8,128)(2,1)S(1)}, f32[512,594]{1,0:T(8,128)S(1)}, bf16[512,594]{1,0:T(8,128)(2...) while((s32[]{:T(128)}, bf16[32,8192]{1,0:T(8,128)(2,1)}, ...), condition=%wide.region_5.6_spmd, body=%wide.region_2.5_spmd.sunk | while | flops 331024288 | bytes 14767196 | solution.py:63
  61.4 9.0 %collective-permute-start = (bf16[32,8192]{1,0:T(8,128)(2,1)}, bf16[32,8192]{1,0:T(8,128)(2,1)S(1)}, u32[]{:S(2)}, u32[]{:S(2)}) collective-permute-start(bf16[32,8192]{1,0:T(8,128)(2,1)} %get-tuple-element.386), channel_id=1, source_target_pairs={{15,0},{0,1},{1,2},{2,3},{3,4},{4,5},{5,6},{6,7},{7,8},{8,9},{9,10... | collective-permute-start | bytes 1572872 | tf_op jit(solution)/shard_map/while/body/eval_jaxpr/ppermute | solution.py:12
  141.1 8.5 %collective-permute-done.1 = bf16[32,512]{1,0:T(8,128)(2,1)S(1)} collective-permute-done((bf16[32,512]{1,0:T(8,128)(2,1)S(1)}, bf16[32,512]{1,0:T(8,128)(2,1)S(1)}, u32[]{:S(2)}, u32[]{:S(2)}) %collective-permute-start.1) | collective-permute-done | bytes 32800 | tf_op jit(solution)/shard_map/while/body/eval_jaxpr/ppermute | solution.py:12
  149.9 6.8 %select_reduce_fusion.6 = (f32[32]{0:T(128)S(1)}, pred[32,594]{1,0:T(8,128)(4,1)S(1)}, f32[32,594]{1,0:T(8,128)S(1)}) fusion(f32[32,594]{1,0:T(8,128)S(1)} %get-tuple-element.362, bf16[32,8192]{1,0:T(8,128)(2,1)S(1)} %collective-permute-done, bf16[8192,594]{0,1:T(8,128)(2,1)} %get-tuple-element.408), kind=kOutput, calls=%fused_computation.1.clone.1 | convolution fusion | flops 311484064 | bytes 10427584 | tf_op jit(solution)/shard_map/while/body/eval_jaxpr/dot_general | solution.py:16
  158.8 10.6 %collective-permute-done.1 = bf16[32,512]{1,0:T(8,128)(2,1)S(1)} collective-permute-done((bf16[32,512]{1,0:T(8,128)(2,1)S(1)}, bf16[32,512]{1,0:T(8,128)(2,1)S(1)}, u32[]{:S(2)}, u32[]{:S(2)}) %collective-permute-start.1) | collective-permute-done | bytes 32800 | tf_op jit(solution)/shard_map/while/body/eval_jaxpr/ppermute | solution.py:12
  169.7 6.8 %select_reduce_fusion.6 = (f32[32]{0:T(128)S(1)}, pred[32,594]{1,0:T(8,128)(4,1)S(1)}, f32[32,594]{1,0:T(8,128)S(1)}) fusion(f32[32,594]{1,0:T(8,128)S(1)} %get-tuple-element.362, bf16[32,8192]{1,0:T(8,128)(2,1)S(1)} %collective-permute-done, bf16[8192,594]{0,1:T(8,128)(2,1)} %get-tuple-element.408), kind=kOutput, calls=%fused_computation.1.clone.1 | convolution fusion | flops 311484064 | bytes 10427584 | tf_op jit(solution)/shard_map/while/body/eval_jaxpr/dot_general | solution.py:16
  177.9 11.3 %collective-permute-done.1 = bf16[32,512]{1,0:T(8,128)(2,1)S(1)} collective-permute-done((bf16[32,512]{1,0:T(8,128)(2,1)S(1)}, bf16[32,512]{1,0:T(8,128)(2,1)S(1)}, u32[]{:S(2)}, u32[]{:S(2)}) %collective-permute-start.1) | collective-permute-done | bytes 32800 | tf_op jit(solution)/shard_map/while/body/eval_jaxpr/ppermute | solution.py:12
  189.5 6.8 %select_reduce_fusion.6 = (f32[32]{0:T(128)S(1)}, pred[32,594]{1,0:T(8,128)(4,1)S(1)}, f32[32,594]{1,0:T(8,128)S(1)}) fusion(f32[32,594]{1,0:T(8,128)S(1)} %get-tuple-element.362, bf16[32,8192]{1,0:T(8,128)(2,1)S(1)} %collective-permute-done, bf16[8192,594]{0,1:T(8,128)(2,1)} %get-tuple-element.408), kind=kOutput, calls=%fused_computation.1.clone.1 | convolution fusion | flops 311484064 | bytes 10427584 | tf_op jit(solution)/shard_map/while/body/eval_jaxpr/dot_general | solution.py:16
  197.7 11.3 %collective-permute-done.1 = bf16[32,512]{1,0:T(8,128)(2,1)S(1)} collective-permute-done((bf16[32,512]{1,0:T(8,128)(2,1)S(1)}, bf16[32,512]{1,0:T(8,128)(2,1)S(1)}, u32[]{:S(2)}, u32[]{:S(2)}) %collective-permute-start.1) | collective-permute-done | bytes 32800 | tf_op jit(solution)/shard_map/while/body/eval_jaxpr/ppermute | solution.py:12
  209.3 6.8 %select_reduce_fusion.6 = (f32[32]{0:T(128)S(1)}, pred[32,594]{1,0:T(8,128)(4,1)S(1)}, f32[32,594]{1,0:T(8,128)S(1)}) fusion(f32[32,594]{1,0:T(8,128)S(1)} %get-tuple-element.362, bf16[32,8192]{1,0:T(8,128)(2,1)S(1)} %collective-permute-done, bf16[8192,594]{0,1:T(8,128)(2,1)} %get-tuple-element.408), kind=kOutput, calls=%fused_computation.1.clone.1 | convolution fusion | flops 311484064 | bytes 10427584 | tf_op jit(solution)/shard_map/while/body/eval_jaxpr/dot_general | solution.py:16
  217.5 11.3 %collective-permute-done.1 = bf16[32,512]{1,0:T(8,128)(2,1)S(1)} collective-permute-done((bf16[32,512]{1,0:T(8,128)(2,1)S(1)}, bf16[32,512]{1,0:T(8,128)(2,1)S(1)}, u32[]{:S(2)}, u32[]{:S(2)}) %collective-permute-start.1) | collective-permute-done | bytes 32800 | tf_op jit(solution)/shard_map/while/body/eval_jaxpr/ppermute | solution.py:12
  229.1 6.8 %select_reduce_fusion.6 = (f32[32]{0:T(128)S(1)}, pred[32,594]{1,0:T(8,128)(4,1)S(1)}, f32[32,594]{1,0:T(8,128)S(1)}) fusion(f32[32,594]{1,0:T(8,128)S(1)} %get-tuple-element.362, bf16[32,8192]{1,0:T(8,128)(2,1)S(1)} %collective-permute-done, bf16[8192,594]{0,1:T(8,128)(2,1)} %get-tuple-element.408), kind=kOutput, calls=%fused_computation.1.clone.1 | convolution fusion | flops 311484064 | bytes 10427584 | tf_op jit(solution)/shard_map/while/body/eval_jaxpr/dot_general | solution.py:16
  237.3 11.3 %collective-permute-done.1 = bf16[32,512]{1,0:T(8,128)(2,1)S(1)} collective-permute-done((bf16[32,512]{1,0:T(8,128)(2,1)S(1)}, bf16[32,512]{1,0:T(8,128)(2,1)S(1)}, u32[]{:S(2)}, u32[]{:S(2)}) %collective-permute-start.1) | collective-permute-done | bytes 32800 | tf_op jit(solution)/shard_map/while/body/eval_jaxpr/ppermute | solution.py:12
  248.9 6.8 %select_reduce_fusion.6 = (f32[32]{0:T(128)S(1)}, pred[32,594]{1,0:T(8,128)(4,1)S(1)}, f32[32,594]{1,0:T(8,128)S(1)}) fusion(f32[32,594]{1,0:T(8,128)S(1)} %get-tuple-element.362, bf16[32,8192]{1,0:T(8,128)(2,1)S(1)} %collective-permute-done, bf16[8192,594]{0,1:T(8,128)(2,1)} %get-tuple-element.408), kind=kOutput, calls=%fused_computation.1.clone.1 | convolution fusion | flops 311484064 | bytes 10427584 | tf_op jit(solution)/shard_map/while/body/eval_jaxpr/dot_general | solution.py:16
  257.1 11.3 %collective-permute-done.1 = bf16[32,512]{1,0:T(8,128)(2,1)S(1)} collective-permute-done((bf16[32,512]{1,0:T(8,128)(2,1)S(1)}, bf16[32,512]{1,0:T(8,128)(2,1)S(1)}, u32[]{:S(2)}, u32[]{:S(2)}) %collective-permute-start.1) | collective-permute-done | bytes 32800 | tf_op jit(solution)/shard_map/while/body/eval_jaxpr/ppermute | solution.py:12
  276.9 11.3 %collective-permute-done.1 = bf16[32,512]{1,0:T(8,128)(2,1)S(1)} collective-permute-done((bf16[32,512]{1,0:T(8,128)(2,1)S(1)}, bf16[32,512]{1,0:T(8,128)(2,1)S(1)}, u32[]{:S(2)}, u32[]{:S(2)}) %collective-permute-start.1) | collective-permute-done | bytes 32800 | tf_op jit(solution)/shard_map/while/body/eval_jaxpr/ppermute | solution.py:12
  288.5 6.8 %select_reduce_fusion.6 = (f32[32]{0:T(128)S(1)}, pred[32,594]{1,0:T(8,128)(4,1)S(1)}, f32[32,594]{1,0:T(8,128)S(1)}) fusion(f32[32,594]{1,0:T(8,128)S(1)} %get-tuple-element.362, bf16[32,8192]{1,0:T(8,128)(2,1)S(1)} %collective-permute-done, bf16[8192,594]{0,1:T(8,128)(2,1)} %get-tuple-element.408), kind=kOutput, calls=%fused_computation.1.clone.1 | convolution fusion | flops 311484064 | bytes 10427584 | tf_op jit(solution)/shard_map/while/body/eval_jaxpr/dot_general | solution.py:16
  296.7 11.3 %collective-permute-done.1 = bf16[32,512]{1,0:T(8,128)(2,1)S(1)} collective-permute-done((bf16[32,512]{1,0:T(8,128)(2,1)S(1)}, bf16[32,512]{1,0:T(8,128)(2,1)S(1)}, u32[]{:S(2)}, u32[]{:S(2)}) %collective-permute-start.1) | collective-permute-done | bytes 32800 | tf_op jit(solution)/shard_map/while/body/eval_jaxpr/ppermute | solution.py:12
  316.5 11.3 %collective-permute-done.1 = bf16[32,512]{1,0:T(8,128)(2,1)S(1)} collective-permute-done((bf16[32,512]{1,0:T(8,128)(2,1)S(1)}, bf16[32,512]{1,0:T(8,128)(2,1)S(1)}, u32[]{:S(2)}, u32[]{:S(2)}) %collective-permute-start.1) | collective-permute-done | bytes 32800 | tf_op jit(solution)/shard_map/while/body/eval_jaxpr/ppermute | solution.py:12
  336.3 11.3 %collective-permute-done.1 = bf16[32,512]{1,0:T(8,128)(2,1)S(1)} collective-permute-done((bf16[32,512]{1,0:T(8,128)(2,1)S(1)}, bf16[32,512]{1,0:T(8,128)(2,1)S(1)}, u32[]{:S(2)}, u32[]{:S(2)}) %collective-permute-start.1) | collective-permute-done | bytes 32800 | tf_op jit(solution)/shard_map/while/body/eval_jaxpr/ppermute | solution.py:12
  357.2 80.2 %pmax.7 = f32[512]{0:T(512)S(1)} all-reduce(f32[512]{0:T(512)S(1)} %get-tuple-element.250), channel_id=1, replica_groups=mesh['rows'=16,'vocab'=16] {'rows','vocab'}, use_global_device_ids=true, to_apply=%region_6.7 | all-reduce | flops 512 | bytes 4096 | tf_op jit(solution)/shard_map/pmax | solution.py:65
  437.4 74.2 %psum.7 = f32[512]{0:T(512)S(1)} all-reduce(f32[512]{0:T(512)S(1)} %exponential_multiply_fusion), channel_id=1, replica_groups=mesh['rows'=16,'vocab'=16] {'rows','vocab'}, use_global_device_ids=true, to_apply=%region_7.8 | all-reduce | flops 512 | bytes 4096 | tf_op jit(solution)/shard_map/psum | solution.py:66
  (171 shorter events, 130.6 us)
Async XLA Ops:
  61.4 15.9 %collective-permute-start = (bf16[32,8192]{1,0:T(8,128)(2,1)}, bf16[32,8192]{1,0:T(8,128)(2,1)S(1)}, u32[]{:S(2)}, u32[]{:S(2)}) collective-permute-start(bf16[32,8192]{1,0:T(8,128)(2,1)} %get-tuple-element.386), channel_id=1, source_target_pairs={{15,0},{0,1},{1,2},{2,3},{3,4},{4,5},{5,6},{6,7},{7,8},{8,9},{9,10... | collective-permute-start | bytes 1572872 | tf_op jit(solution)/shard_map/while/body/eval_jaxpr/ppermute | solution.py:12
  85.6 9.4 %collective-permute-start = (bf16[32,8192]{1,0:T(8,128)(2,1)}, bf16[32,8192]{1,0:T(8,128)(2,1)S(1)}, u32[]{:S(2)}, u32[]{:S(2)}) collective-permute-start(bf16[32,8192]{1,0:T(8,128)(2,1)} %get-tuple-element.386), channel_id=1, source_target_pairs={{15,0},{0,1},{1,2},{2,3},{3,4},{4,5},{5,6},{6,7},{7,8},{8,9},{9,10... | collective-permute-start | bytes 1572872 | tf_op jit(solution)/shard_map/while/body/eval_jaxpr/ppermute | solution.py:12
  103.2 9.4 %collective-permute-start = (bf16[32,8192]{1,0:T(8,128)(2,1)}, bf16[32,8192]{1,0:T(8,128)(2,1)S(1)}, u32[]{:S(2)}, u32[]{:S(2)}) collective-permute-start(bf16[32,8192]{1,0:T(8,128)(2,1)} %get-tuple-element.386), channel_id=1, source_target_pairs={{15,0},{0,1},{1,2},{2,3},{3,4},{4,5},{5,6},{6,7},{7,8},{8,9},{9,10... | collective-permute-start | bytes 1572872 | tf_op jit(solution)/shard_map/while/body/eval_jaxpr/ppermute | solution.py:12
  138.6 11.3 %collective-permute-start = (bf16[32,8192]{1,0:T(8,128)(2,1)}, bf16[32,8192]{1,0:T(8,128)(2,1)S(1)}, u32[]{:S(2)}, u32[]{:S(2)}) collective-permute-start(bf16[32,8192]{1,0:T(8,128)(2,1)} %get-tuple-element.386), channel_id=1, source_target_pairs={{15,0},{0,1},{1,2},{2,3},{3,4},{4,5},{5,6},{6,7},{7,8},{8,9},{9,10... | collective-permute-start | bytes 1572872 | tf_op jit(solution)/shard_map/while/body/eval_jaxpr/ppermute | solution.py:12
  158.1 11.5 %collective-permute-start = (bf16[32,8192]{1,0:T(8,128)(2,1)}, bf16[32,8192]{1,0:T(8,128)(2,1)S(1)}, u32[]{:S(2)}, u32[]{:S(2)}) collective-permute-start(bf16[32,8192]{1,0:T(8,128)(2,1)} %get-tuple-element.386), channel_id=1, source_target_pairs={{15,0},{0,1},{1,2},{2,3},{3,4},{4,5},{5,6},{6,7},{7,8},{8,9},{9,10... | collective-permute-start | bytes 1572872 | tf_op jit(solution)/shard_map/while/body/eval_jaxpr/ppermute | solution.py:12
  158.8 10.6 %collective-permute-start.1 = (bf16[32,512]{1,0:T(8,128)(2,1)S(1)}, bf16[32,512]{1,0:T(8,128)(2,1)S(1)}, u32[]{:S(2)}, u32[]{:S(2)}) collective-permute-start(bf16[32,512]{1,0:T(8,128)(2,1)S(1)} %get-tuple-element.387), channel_id=1, source_target_pairs={{15,0},{0,1},{1,2},{2,3},{3,4},{4,5},{5,6},{6,7},{7,8},{8,9},{9,10... | collective-permute-start | bytes 98312 | tf_op jit(solution)/shard_map/while/body/eval_jaxpr/ppermute | solution.py:12
  177.9 11.5 %collective-permute-start = (bf16[32,8192]{1,0:T(8,128)(2,1)}, bf16[32,8192]{1,0:T(8,128)(2,1)S(1)}, u32[]{:S(2)}, u32[]{:S(2)}) collective-permute-start(bf16[32,8192]{1,0:T(8,128)(2,1)} %get-tuple-element.386), channel_id=1, source_target_pairs={{15,0},{0,1},{1,2},{2,3},{3,4},{4,5},{5,6},{6,7},{7,8},{8,9},{9,10... | collective-permute-start | bytes 1572872 | tf_op jit(solution)/shard_map/while/body/eval_jaxpr/ppermute | solution.py:12
  177.9 11.3 %collective-permute-start.1 = (bf16[32,512]{1,0:T(8,128)(2,1)S(1)}, bf16[32,512]{1,0:T(8,128)(2,1)S(1)}, u32[]{:S(2)}, u32[]{:S(2)}) collective-permute-start(bf16[32,512]{1,0:T(8,128)(2,1)S(1)} %get-tuple-element.387), channel_id=1, source_target_pairs={{15,0},{0,1},{1,2},{2,3},{3,4},{4,5},{5,6},{6,7},{7,8},{8,9},{9,10... | collective-permute-start | bytes 98312 | tf_op jit(solution)/shard_map/while/body/eval_jaxpr/ppermute | solution.py:12
  197.7 11.5 %collective-permute-start = (bf16[32,8192]{1,0:T(8,128)(2,1)}, bf16[32,8192]{1,0:T(8,128)(2,1)S(1)}, u32[]{:S(2)}, u32[]{:S(2)}) collective-permute-start(bf16[32,8192]{1,0:T(8,128)(2,1)} %get-tuple-element.386), channel_id=1, source_target_pairs={{15,0},{0,1},{1,2},{2,3},{3,4},{4,5},{5,6},{6,7},{7,8},{8,9},{9,10... | collective-permute-start | bytes 1572872 | tf_op jit(solution)/shard_map/while/body/eval_jaxpr/ppermute | solution.py:12
  197.7 11.3 %collective-permute-start.1 = (bf16[32,512]{1,0:T(8,128)(2,1)S(1)}, bf16[32,512]{1,0:T(8,128)(2,1)S(1)}, u32[]{:S(2)}, u32[]{:S(2)}) collective-permute-start(bf16[32,512]{1,0:T(8,128)(2,1)S(1)} %get-tuple-element.387), channel_id=1, source_target_pairs={{15,0},{0,1},{1,2},{2,3},{3,4},{4,5},{5,6},{6,7},{7,8},{8,9},{9,10... | collective-permute-start | bytes 98312 | tf_op jit(solution)/shard_map/while/body/eval_jaxpr/ppermute | solution.py:12
  217.5 11.5 %collective-permute-start = (bf16[32,8192]{1,0:T(8,128)(2,1)}, bf16[32,8192]{1,0:T(8,128)(2,1)S(1)}, u32[]{:S(2)}, u32[]{:S(2)}) collective-permute-start(bf16[32,8192]{1,0:T(8,128)(2,1)} %get-tuple-element.386), channel_id=1, source_target_pairs={{15,0},{0,1},{1,2},{2,3},{3,4},{4,5},{5,6},{6,7},{7,8},{8,9},{9,10... | collective-permute-start | bytes 1572872 | tf_op jit(solution)/shard_map/while/body/eval_jaxpr/ppermute | solution.py:12
  217.5 11.3 %collective-permute-start.1 = (bf16[32,512]{1,0:T(8,128)(2,1)S(1)}, bf16[32,512]{1,0:T(8,128)(2,1)S(1)}, u32[]{:S(2)}, u32[]{:S(2)}) collective-permute-start(bf16[32,512]{1,0:T(8,128)(2,1)S(1)} %get-tuple-element.387), channel_id=1, source_target_pairs={{15,0},{0,1},{1,2},{2,3},{3,4},{4,5},{5,6},{6,7},{7,8},{8,9},{9,10... | collective-permute-start | bytes 98312 | tf_op jit(solution)/shard_map/while/body/eval_jaxpr/ppermute | solution.py:12
  237.3 11.5 %collective-permute-start = (bf16[32,8192]{1,0:T(8,128)(2,1)}, bf16[32,8192]{1,0:T(8,128)(2,1)S(1)}, u32[]{:S(2)}, u32[]{:S(2)}) collective-permute-start(bf16[32,8192]{1,0:T(8,128)(2,1)} %get-tuple-element.386), channel_id=1, source_target_pairs={{15,0},{0,1},{1,2},{2,3},{3,4},{4,5},{5,6},{6,7},{7,8},{8,9},{9,10... | collective-permute-start | bytes 1572872 | tf_op jit(solution)/shard_map/while/body/eval_jaxpr/ppermute | solution.py:12
  237.3 11.3 %collective-permute-start.1 = (bf16[32,512]{1,0:T(8,128)(2,1)S(1)}, bf16[32,512]{1,0:T(8,128)(2,1)S(1)}, u32[]{:S(2)}, u32[]{:S(2)}) collective-permute-start(bf16[32,512]{1,0:T(8,128)(2,1)S(1)} %get-tuple-element.387), channel_id=1, source_target_pairs={{15,0},{0,1},{1,2},{2,3},{3,4},{4,5},{5,6},{6,7},{7,8},{8,9},{9,10... | collective-permute-start | bytes 98312 | tf_op jit(solution)/shard_map/while/body/eval_jaxpr/ppermute | solution.py:12
  257.1 11.5 %collective-permute-start = (bf16[32,8192]{1,0:T(8,128)(2,1)}, bf16[32,8192]{1,0:T(8,128)(2,1)S(1)}, u32[]{:S(2)}, u32[]{:S(2)}) collective-permute-start(bf16[32,8192]{1,0:T(8,128)(2,1)} %get-tuple-element.386), channel_id=1, source_target_pairs={{15,0},{0,1},{1,2},{2,3},{3,4},{4,5},{5,6},{6,7},{7,8},{8,9},{9,10... | collective-permute-start | bytes 1572872 | tf_op jit(solution)/shard_map/while/body/eval_jaxpr/ppermute | solution.py:12
  257.1 11.3 %collective-permute-start.1 = (bf16[32,512]{1,0:T(8,128)(2,1)S(1)}, bf16[32,512]{1,0:T(8,128)(2,1)S(1)}, u32[]{:S(2)}, u32[]{:S(2)}) collective-permute-start(bf16[32,512]{1,0:T(8,128)(2,1)S(1)} %get-tuple-element.387), channel_id=1, source_target_pairs={{15,0},{0,1},{1,2},{2,3},{3,4},{4,5},{5,6},{6,7},{7,8},{8,9},{9,10... | collective-permute-start | bytes 98312 | tf_op jit(solution)/shard_map/while/body/eval_jaxpr/ppermute | solution.py:12
  276.9 11.5 %collective-permute-start = (bf16[32,8192]{1,0:T(8,128)(2,1)}, bf16[32,8192]{1,0:T(8,128)(2,1)S(1)}, u32[]{:S(2)}, u32[]{:S(2)}) collective-permute-start(bf16[32,8192]{1,0:T(8,128)(2,1)} %get-tuple-element.386), channel_id=1, source_target_pairs={{15,0},{0,1},{1,2},{2,3},{3,4},{4,5},{5,6},{6,7},{7,8},{8,9},{9,10... | collective-permute-start | bytes 1572872 | tf_op jit(solution)/shard_map/while/body/eval_jaxpr/ppermute | solution.py:12
  276.9 11.3 %collective-permute-start.1 = (bf16[32,512]{1,0:T(8,128)(2,1)S(1)}, bf16[32,512]{1,0:T(8,128)(2,1)S(1)}, u32[]{:S(2)}, u32[]{:S(2)}) collective-permute-start(bf16[32,512]{1,0:T(8,128)(2,1)S(1)} %get-tuple-element.387), channel_id=1, source_target_pairs={{15,0},{0,1},{1,2},{2,3},{3,4},{4,5},{5,6},{6,7},{7,8},{8,9},{9,10... | collective-permute-start | bytes 98312 | tf_op jit(solution)/shard_map/while/body/eval_jaxpr/ppermute | solution.py:12
  296.7 11.5 %collective-permute-start = (bf16[32,8192]{1,0:T(8,128)(2,1)}, bf16[32,8192]{1,0:T(8,128)(2,1)S(1)}, u32[]{:S(2)}, u32[]{:S(2)}) collective-permute-start(bf16[32,8192]{1,0:T(8,128)(2,1)} %get-tuple-element.386), channel_id=1, source_target_pairs={{15,0},{0,1},{1,2},{2,3},{3,4},{4,5},{5,6},{6,7},{7,8},{8,9},{9,10... | collective-permute-start | bytes 1572872 | tf_op jit(solution)/shard_map/while/body/eval_jaxpr/ppermute | solution.py:12
  296.7 11.3 %collective-permute-start.1 = (bf16[32,512]{1,0:T(8,128)(2,1)S(1)}, bf16[32,512]{1,0:T(8,128)(2,1)S(1)}, u32[]{:S(2)}, u32[]{:S(2)}) collective-permute-start(bf16[32,512]{1,0:T(8,128)(2,1)S(1)} %get-tuple-element.387), channel_id=1, source_target_pairs={{15,0},{0,1},{1,2},{2,3},{3,4},{4,5},{5,6},{6,7},{7,8},{8,9},{9,10... | collective-permute-start | bytes 98312 | tf_op jit(solution)/shard_map/while/body/eval_jaxpr/ppermute | solution.py:12
  316.5 11.5 %collective-permute-start = (bf16[32,8192]{1,0:T(8,128)(2,1)}, bf16[32,8192]{1,0:T(8,128)(2,1)S(1)}, u32[]{:S(2)}, u32[]{:S(2)}) collective-permute-start(bf16[32,8192]{1,0:T(8,128)(2,1)} %get-tuple-element.386), channel_id=1, source_target_pairs={{15,0},{0,1},{1,2},{2,3},{3,4},{4,5},{5,6},{6,7},{7,8},{8,9},{9,10... | collective-permute-start | bytes 1572872 | tf_op jit(solution)/shard_map/while/body/eval_jaxpr/ppermute | solution.py:12
  316.5 11.3 %collective-permute-start.1 = (bf16[32,512]{1,0:T(8,128)(2,1)S(1)}, bf16[32,512]{1,0:T(8,128)(2,1)S(1)}, u32[]{:S(2)}, u32[]{:S(2)}) collective-permute-start(bf16[32,512]{1,0:T(8,128)(2,1)S(1)} %get-tuple-element.387), channel_id=1, source_target_pairs={{15,0},{0,1},{1,2},{2,3},{3,4},{4,5},{5,6},{6,7},{7,8},{8,9},{9,10... | collective-permute-start | bytes 98312 | tf_op jit(solution)/shard_map/while/body/eval_jaxpr/ppermute | solution.py:12
  336.3 11.5 %collective-permute-start = (bf16[32,8192]{1,0:T(8,128)(2,1)}, bf16[32,8192]{1,0:T(8,128)(2,1)S(1)}, u32[]{:S(2)}, u32[]{:S(2)}) collective-permute-start(bf16[32,8192]{1,0:T(8,128)(2,1)} %get-tuple-element.386), channel_id=1, source_target_pairs={{15,0},{0,1},{1,2},{2,3},{3,4},{4,5},{5,6},{6,7},{7,8},{8,9},{9,10... | collective-permute-start | bytes 1572872 | tf_op jit(solution)/shard_map/while/body/eval_jaxpr/ppermute | solution.py:12
  336.3 11.3 %collective-permute-start.1 = (bf16[32,512]{1,0:T(8,128)(2,1)S(1)}, bf16[32,512]{1,0:T(8,128)(2,1)S(1)}, u32[]{:S(2)}, u32[]{:S(2)}) collective-permute-start(bf16[32,512]{1,0:T(8,128)(2,1)S(1)} %get-tuple-element.387), channel_id=1, source_target_pairs={{15,0},{0,1},{1,2},{2,3},{3,4},{4,5},{5,6},{6,7},{7,8},{8,9},{9,10... | collective-permute-start | bytes 98312 | tf_op jit(solution)/shard_map/while/body/eval_jaxpr/ppermute | solution.py:12
  (9 other events, 201.8 us)
where the time goes:
time: 514 us; the launch traced here: 513 us
  blocking collectives  198 us (39%)
  waiting for transfers between devices  147 us (29%)
  matrix products  113 us (22%)
  local copies, waits for them, and re-layouts  29.9 us (6%)
  starting transfers between devices  19.7 us (4%)
  other arithmetic  5.2 us (1%)
    ppermute x30, waiting for transfers between devices, passed_along(): return lax.ppermute(block, axis, route)  147 us
    dot_general x16, matrix products, stop_parts(): logits = jnp.dot(row_block, head_weight, preferred_element_type=jnp.float32)  109 us
    pmax x1, blocking collectives, local(): row_peak = lax.pmax(peak_buf, ('rows', 'vocab'))  80.2 us
    psum x1, blocking collectives, local(): lax.psum(total_buf * jnp.exp(peak_buf - row_peak), ('rows', 'vocab'))  74.2 us
    all_gather x1, blocking collectives, local(): row_block = lax.all_gather(hidden_rows, 'rows', axis=1, tiled=True)  43.1 us
    ppermute x30, starting transfers between devices, passed_along(): return lax.ppermute(block, axis, route)  19.7 us
    while x30, local copies, waits for them, and re-layouts  11.9 us
  transfers between devices with their start and end apart: 30, of which 15 were waited for; matrix products, arithmetic and copies ran while one was open for 1% of the time, Pallas kernels for 0%

commit v1 on v0

v1 whole, which is shorter than its diff:
```python
import jax
import jax.numpy as jnp
from jax import lax
from jax.sharding import PartitionSpec as P

lowest = -1e30


def local(hidden_rows, row_states, head_weight, grammar_table):
    state_count = grammar_table.shape[0]
    block = lax.all_gather(hidden_rows, "vocab", axis=0, tiled=True)
    states = lax.all_gather(row_states, "vocab", axis=0, tiled=True)
    every = lax.all_gather(block, "rows", axis=1, tiled=True)
    onehot = (jnp.arange(state_count, dtype=jnp.int32)[:, None] == states[None, :]).astype(jnp.bfloat16)
    allowed = (
        lax.dot_general(
            grammar_table.astype(jnp.bfloat16),
            onehot,
            (((0,), (0,)), ((), ())),
            preferred_element_type=jnp.float32,
        )
        > 0.5
    )
    logits = lax.dot_general(
        head_weight, every, (((0,), (1,)), ((), ())), preferred_element_type=jnp.float32
    )
    masked = jnp.where(allowed, logits, lowest)
    own_peak = jnp.max(masked, axis=0)
    own_total = jnp.sum(jnp.where(allowed, jnp.exp(masked - own_peak[None, :]), 0.0), axis=0)
    row_peak = lax.pmax(own_peak, ("rows", "vocab"))
    exp_total = lax.psum(own_total * jnp.exp(own_peak - row_peak), ("rows", "vocab"))
    normalizer = row_peak + jnp.log(exp_total)
    log_probs = jnp.where(allowed, logits - normalizer[None, :], 0.0)
    return (log_probs.T, normalizer)


def solution(mesh):
    placed = (
        P("vocab", "rows"),
        P("vocab"),
        P(None, ("rows", "vocab")),
        P(None, ("rows", "vocab")),
    )
    return jax.shard_map(
        local,
        mesh=mesh,
        in_specs=placed,
        out_specs=(P(None, ("rows", "vocab")), P()),
        check_vma=False,
    )
```

time: 514 us -> 345 us (0.67)
  matrix products: 113 us -> 12.4 us
  local copies, waits for them, and re-layouts: 29.9 us -> 2.13 us
  starting transfers between devices: 19.7 us -> 0.04 us
  blocking collectives: 198 us -> 181 us
  waiting for transfers between devices: 147 us -> 133 us
  between operations: 0.72 us -> 14.7 us
    ppermute x30 -> x0, waiting for transfers between devices: 147 us -> none  [passed_along(): return lax.ppermute(block, axis, route)]
    all_gather x0 -> x1, waiting for transfers between devices: none -> 133 us  [local(): every = lax.all_gather(block, 'rows', axis=1, tiled=True)]
    dot_general x32 -> x2, matrix products: 113 us -> 12.4 us  [the longest x1 10.5 us: local(): lax.dot_general(head_weight, every, (((0,), (1,)), ((), ())), preferred_e...]
    ppermute x30 -> x0, starting transfers between devices: 19.7 us -> none  [passed_along(): return lax.ppermute(block, axis, route)]
    all_gather x1, blocking collectives: 43.1 us -> 24.3 us  [local(): block = lax.all_gather(hidden_rows, 'vocab', axis=0, tiled=True)]
    while x33 -> x0, local copies, waits for them, and re-layouts: 15 us -> none
    dynamic_update_slice x33 -> x0, local copies, waits for them, and re-layouts: 11.3 us -> none  [the longest x16 3.89 us: record(): peak_buf = lax.dynamic_update_slice_in_dim(peak_buf, row_peak, row_start, 0)]
    unnamed x0 -> x1, blocking collectives: none -> 5.89 us
  transfers between devices with their start and end apart: 30 -> 1, of which waited for: 15 -> 1; matrix products, arithmetic and copies ran while one was open for 1% -> 1% of each run, Pallas kernels for 0% -> 0%
where the time goes in v1:
time: 345 us
  blocking collectives  181 us (52%)
  waiting for transfers between devices  133 us (39%)
  between operations  14.7 us (4%)
  matrix products  12.4 us (4%)
    all_gather x1, waiting for transfers between devices, local(): every = lax.all_gather(block, 'rows', axis=1, tiled=True)  133 us
    pmax x1, blocking collectives, local(): row_peak = lax.pmax(own_peak, ('rows', 'vocab'))  78.6 us
    psum x1, blocking collectives, local(): lax.psum(own_total * jnp.exp(own_peak - row_peak), ('rows', 'vocab'))  72.4 us
    all_gather x1, blocking collectives, local(): block = lax.all_gather(hidden_rows, 'vocab', axis=0, tiled=True)  24.3 us
    dot_general x1, matrix products, local(): lax.dot_general(head_weight, every, (((0,), (1,)), ((), ())), preferred_e...  10.5 us
  transfers between devices with their start and end apart: 1, of which 1 were waited for; matrix products, arithmetic and copies ran while one was open for 1% of the time, Pallas kernels for 0%

profile of v1, /device:TPU:1, one launch (start us, length us, event | category | flops | bytes accessed | tf_op | source)
XLA Modules:
  0.0 344.6 jit_solution(1174244947708664710)
XLA Ops:
  7.2 0.0 all-gather.2.cloned.1.call-start
  7.2 24.3 %all_gather.10 = bf16[512,512]{1,0:T(8,128)(2,1)} all-gather(bf16[32,512]{1,0:T(8,128)(2,1)} %param.4), channel_id=1, replica_groups=mesh['rows'=16,'vocab'=16] {'vocab'}, dimensions={0}, use_global_device_ids=true | all-gather | bytes 557056 | tf_op jit(solution)/shard_map/all_gather | solution.py:11
  31.5 0.0 all-gather.2.cloned.1.call-update
  31.5 1.3 dynamic-slice
  33.4 0.9 dynamic-update-slice
  34.3 5.9 %all-reduce = s32[512]{0:T(512)S(1)} all-reduce(s32[512]{0:T(512)S(1)} %dynamic-update-slice), channel_id=1, replica_groups=mesh['rows'=16,'vocab'=16] {'vocab'}, use_global_device_ids=true, to_apply=%add | all-reduce | flops 512 | bytes 4096
  40.2 1.8 convolution_compare_fusion
  42.0 132.7 %all-gather.2.cloned.1.call-done = bf16[512,8192]{1,0:T(8,128)(2,1)} async-done(((bf16[512,512]{1,0:T(8,128)(2,1)}), bf16[512,8192]{1,0:T(8,128)(2,1)}) %all-gather.2.cloned.1.call-update) | async-done | bytes 8388624 | tf_op jit(solution)/shard_map/all_gather | solution.py:13
  174.7 10.5 %fusion = (f32[512]{0:T(512)S(1)}, f32[594,512]{1,0:T(8,128)S(1)}) fusion(pred[512,594]{0,1:T(8,128)(4,1)S(1)} %convolution_compare_fusion, bf16[8192,594]{0,1:T(8,128)(2,1)} %param.6, bf16[512,8192]{1,0:T(8,128)(2,1)} %all-gather.2.cloned.1.call-done), kind=kOutput, calls=%fused_computation.4 | convolution fusion | flops 4983440896 | bytes 19643392 | tf_op jit(solution)/shard_map/dot_general | solution.py:24
  185.2 78.6 %pmax.7 = f32[512]{0:T(512)S(1)} all-reduce(f32[512]{0:T(512)S(1)} %get-tuple-element.2), channel_id=1, replica_groups=mesh['rows'=16,'vocab'=16] {'rows','vocab'}, use_global_device_ids=true, to_apply=%region_1.2 | all-reduce | flops 512 | bytes 4096 | tf_op jit(solution)/shard_map/pmax | solution.py:30
  263.8 0.4 select_reduce_fusion
  264.1 72.4 %psum.7 = f32[512]{0:T(512)S(1)} all-reduce(f32[512]{0:T(512)S(1)} %exponential_multiply_fusion), channel_id=1, replica_groups=mesh['rows'=16,'vocab'=16] {'rows','vocab'}, use_global_device_ids=true, to_apply=%region_3.4 | all-reduce | flops 512 | bytes 4096 | tf_op jit(solution)/shard_map/psum | solution.py:31
  336.5 0.0 copy-start
  336.5 1.3 bitcast_select_fusion
  337.8 0.0 copy-done
  (3 shorter events, 0.0 us)
Async XLA Ops:
  7.2 167.5 %all-gather.2.cloned.1.call-start = ((), (), s32[]{:S(2)}) async-start(), calls=%async_computation | async-start | bytes 8912896 | tf_op jit(solution)/shard_map/all_gather | solution.py:13
  336.5 1.3 copy-start
Sparse Core Ops, SparseCore 0:
  31.6 143.0 all-gather.1

commit v2 on v1

v2 whole, which is shorter than its diff:
```python
import functools
import heapq
import itertools

import jax
import jax.numpy as jnp
from jax import lax
from jax.experimental import pallas as pl
from jax.experimental.pallas import tpu as pltpu
from jax.sharding import PartitionSpec as P

LOWEST = -1e30
NX, NY, NZ = 4, 4, 8
MESH = pl.DeviceIdType.MESH
HOP = 1.0
RATE = 46e3
NT = (((1,), (1,)), ((), ()))


def place(x, y, z, c):
    rows = z * 2 + lax.div(x, 2)
    vocab = lax.rem(x, 2) * 8 + y * 2 + c
    return (rows, vocab)


def b_first(z):
    return lax.div(z, 4) * 6 + lax.rem(z, 4)


def b_second(z):
    even = lax.div(z, 4) * 6 + 4 + lax.div(lax.rem(z, 4), 2)
    return jnp.where(lax.rem(z, 2) == 0, even, 12 + lax.div(z, 2))


def c_second(z):
    return jnp.where(lax.rem(z, 2) == 1, 8, 12) + lax.div(z, 2)


def kernel(
    hid, st_in, w_in, tab_in, acc_out, norm_out,
    ha, hb, hc, st, w, tab, ls, send, recv, near_send, near_recv, local,
):
    r, v = lax.axis_index("rows"), lax.axis_index("vocab")
    z, x = lax.div(r, 2), lax.rem(r, 2) * 2 + lax.div(v, 8)
    y, c = lax.rem(lax.div(v, 2), NY), lax.rem(v, 2)
    other = 1 - c
    columns = w_in.shape[0]

    def along(axis, step):
        size = {"x": NX, "y": NY, "z": NZ}[axis]
        at = {"x": x, "y": y, "z": z}
        at[axis] = lax.rem(at[axis] + size + step, size)
        return place(at["x"], at["y"], at["z"], c)

    partner = place(x, y, z, other)
    x_lo = lax.rem(x, 2)
    x_flip = place(x + 1 - 2 * x_lo, y, z, c)

    fills = []

    def fill(source, target):
        copy = pltpu.make_async_copy(source, target, local.at[len(fills)])
        copy.start()
        fills.append(copy)
        return copy

    quarter = [hid.at[:, pl.ds(128 * q, 128)] for q in range(4)]
    fill(quarter[0], ha.at[c, z, y, x])
    fill(quarter[1], hb.at[c, x, b_first(z), y])
    fill(quarter[2], hb.at[c, x, b_second(z), y])
    fill(quarter[3], hc.at[c, y, x, z])
    fill(quarter[2], hc.at[c, y, x, c_second(z)])
    fill(st_in, st.at[c, y, x_lo])
    tab_fill = fill(tab_in, tab)
    w_fill = fill(w_in, w)

    barrier = pltpu.get_barrier_semaphore()
    friends = [along(a, s) for a in "xyz" for s in (1, -1)] + [partner]
    for friend in friends:
        pl.semaphore_signal(barrier, inc=1, device_id=friend, device_id_type=MESH)
    pl.semaphore_wait(barrier, len(friends))
    for copy in fills[:6]:
        copy.wait()

    count = itertools.count()
    near_count = itertools.count()
    sent = []

    def remote(source, device, index, sends, recvs):
        copy = pltpu.make_async_remote_copy(
            src_ref=source, dst_ref=source, send_sem=sends.at[index],
            recv_sem=recvs.at[index], device_id=device, device_id_type=MESH,
        )
        copy.start()
        sent.append(copy)

    def arrived(target, index, recvs):
        pltpu.make_async_copy(target, target, recvs.at[index]).wait()

    def ring(axis, size, pos, piece, nbytes, start, seen):
        half = size // 2
        index = {}
        for d in range(1, half + 1):
            for way in (1, -1):
                for h in (0, 1):
                    if d < half or h == (0 if way > 0 else 1):
                        index[way, d, h] = next(count)
        step = nbytes / RATE
        when = {}
        for way in (1, -1):
            order = (0, 1) if way > 0 else (1, 0)
            for h in order:
                remote(piece(pos, h), along(axis, way), index[way, 1, h], send, recv)
            free = start
            for d in range(1, half + 1):
                for h in order:
                    if (way, d, h) in index:
                        ready = start if d == 1 else when[way, d - 1, h]
                        free = max(free, ready) + step
                        when[way, d, h] = free + HOP
        for key in sorted(index, key=lambda k: (when[k], k[1], -k[0])):
            way, d, h = key
            yield when[key]
            origin = lax.rem(pos + size - way * d, size)
            arrived(piece(origin, h), index[key], recv)
            if (way, d + 1, h) in index:
                remote(piece(origin, h), along(axis, way), index[way, d + 1, h], send, recv)
            seen(way, d, h, origin, when[key])
        return max(when.values())

    def ignore(*_):
        return None

    queue = []
    order = itertools.count()

    def push(time, action):
        heapq.heappush(queue, (time, next(order), action))

    def drive(generator):
        def action():
            try:
                time = next(generator)
            except StopIteration:
                return
            push(time, action)

        action()

    waits = {}

    def hand_over(name, piece, pos, h, time, key, nbytes):
        index = next(near_count)
        remote(piece(c, pos, h), partner, index, near_send, near_recv)
        waits[name, key, h] = (piece(other, pos, h), index, time + 1.0 + nbytes / 2e5)
        return waits[name, key, h][2]

    def gather(name, phases, piece, nbytes, done):
        start = 0.0
        for number, (axis, size, pos, part, part_bytes) in enumerate(phases):
            last = number == len(phases) - 1
            if last:
                for h in (0, 1):
                    ready = hand_over(name, piece, pos, h, start, (0, 0), nbytes)
                    done((0, 0), h, pos, ready)

                def seen(way, d, h, origin, time):
                    key = (way, d) if d < size // 2 else (0, d)
                    ready = hand_over(name, piece, origin, h, time, key, nbytes)
                    done(key, h, origin, ready)
            else:
                seen = ignore
            start = yield from ring(axis, size, pos, part, part_bytes, start, seen)

    def received(name, key, h):
        target, index, _ = waits[name, key, h]
        arrived(target, index, near_recv)

    block = 32 * 128 * 2
    a_piece = lambda core, p, h: ha.at[core, p, pl.ds(2 * h, 2)]
    b_piece = lambda core, p, h: hb.at[core, p, pl.ds(6 * h, 6)]
    c_piece = lambda core, p, h: hc.at[core, p, pl.ds(2 * h, 2), pl.ds(0, 12)]

    def weights(offsets):
        return jnp.concatenate(
            [w[:, pl.ds(pl.multiple_of(o, 128), 128)] for o in offsets], axis=1
        )

    def stack(parts):
        return jnp.concatenate(parts, axis=0)

    def a_task(zz):
        rhs = jnp.concatenate(
            [
                stack(
                    [
                        ha[core, zz, yy, 2 * hi + lo]
                        for lo in range(2) for yy in range(NY) for core in range(2)
                    ]
                )
                for hi in range(2)
            ],
            axis=1,
        )
        lhs = weights([(2 * zz + hi) * 512 for hi in range(2)])
        acc_out[...] += lax.dot_general(lhs, rhs, NT, preferred_element_type=jnp.float32)

    def b_task(xx, h):
        hi, lo = lax.div(xx, 2), lax.rem(xx, 2)
        rhs = jnp.concatenate(
            [
                stack([hb[core, xx, 6 * h + s, yy] for yy in range(NY) for core in range(2)])
                for s in range(6)
            ],
            axis=1,
        )
        offsets = [(2 * (4 * h + s) + hi) * 512 + 128 for s in range(4)]
        offsets += [(2 * (4 * h + 2 * s) + hi) * 512 + 256 for s in range(2)]
        lanes = pl.ds(pl.multiple_of(lo * 256, 128), 256)
        acc_out[:, lanes] += lax.dot_general(
            weights(offsets), rhs, NT, preferred_element_type=jnp.float32
        )

    def c_task(pair, h):
        rhs = jnp.concatenate(
            [
                stack(
                    [
                        hc[core, 2 * pair + yy, 2 * h + lo, s]
                        for lo in range(2) for yy in range(2) for core in range(2)
                    ]
                )
                for s in range(12)
            ],
            axis=1,
        )
        offsets = [(2 * s + h) * 512 + 384 for s in range(8)]
        offsets += [(2 * (2 * s + 1) + h) * 512 + 256 for s in range(4)]
        out = lax.dot_general(weights(offsets), rhs, NT, preferred_element_type=jnp.float32)
        for lo in range(2):
            lanes = pl.ds(pl.multiple_of(lo * 256 + pair * 128, 128), 128)
            acc_out[:, lanes] += out[:, lo * 128 : (lo + 1) * 128]

    have = {}

    def a_done(key, h, origin, ready):
        have["a", key, h] = ready
        if ("a", key, 1 - h) in have:
            def action():
                for half in (0, 1):
                    received("a", key, half)
                a_task(origin)
            push(max(ready, have["a", key, 1 - h]), action)

    def b_done(key, h, origin, ready):
        def action():
            received("b", key, h)
            b_task(origin, h)
        push(ready, action)

    def c_done(key, h, origin, ready):
        have["c", key, h] = ready
        near = [(0, 0), (1, 1), (-1, 1)]
        if key in near and all(("c", k, h) in have for k in near):
            def action():
                for k in near:
                    received("c", k, h)
                c_task(lax.div(y, 2), h)
            push(max(have["c", k, h] for k in near), action)
        if key == (0, 2):
            def action():
                received("c", key, h)
                c_task(1 - lax.div(y, 2), h)
            push(ready, action)

    def states():
        index = [next(count) for _ in range(4)]
        remote(st.at[c, y, x_lo], x_flip, index[0], send, recv)
        yield 1.5
        arrived(st.at[c, y, 1 - x_lo], index[0], recv)
        for way, k in ((1, 1), (-1, 2)):
            remote(st.at[c, y], along("y", way), index[k], send, recv)
        yield 3.0
        below, above = lax.rem(y + 3, NY), lax.rem(y + 1, NY)
        arrived(st.at[c, below], index[1], recv)
        remote(st.at[c, below], along("y", 1), index[3], send, recv)
        yield 3.1
        arrived(st.at[c, above], index[2], recv)
        yield 4.5
        arrived(st.at[c, lax.rem(y + 2, NY)], index[3], recv)
        near = next(near_count)
        remote(st.at[c], partner, near, near_send, near_recv)
        yield 6.0
        arrived(st.at[other], near, near_recv)
        tab_fill.wait()
        group = lax.div(lax.broadcasted_iota(jnp.int32, (1, 128), 1), 32)
        parts = []
        for lo in range(2):
            for pair in range(2):
                picked = st[1, 2 * pair + 1, lo, 0:1]
                for k in range(3):
                    picked = jnp.where(group == k, st[k % 2, 2 * pair + k // 2, lo, 0:1], picked)
                parts.append(picked)
        row_states = jnp.concatenate(parts, axis=1)
        marks = lax.broadcasted_iota(jnp.int32, (tab.shape[1], row_states.shape[1]), 0)
        onehot = jnp.where(marks == row_states, 1.0, 0.0).astype(jnp.bfloat16)
        allowed = jnp.dot(
            tab[...].astype(jnp.float32).astype(jnp.bfloat16), onehot, preferred_element_type=jnp.float32
        )
        acc_out[...] = jnp.where(allowed > 0.5, 0.0, LOWEST)
        w_fill.wait()

    drive(states())
    drive(
        gather(
            "c",
            [
                ("z", NZ, z, lambda p, h: hc.at[c, y, x, p if h == 0 else c_second(p)], block),
                ("x", NX, x, lambda p, h: hc.at[c, y, p, pl.ds(6 * h, 6)], 6 * block),
                ("y", NY, y, lambda p, h: c_piece(c, p, h), 24 * block),
            ],
            c_piece, 24 * block, c_done,
        )
    )
    drive(
        gather(
            "b",
            [
                ("y", NY, y, lambda p, h: hb.at[c, x, b_first(z) if h == 0 else b_second(z), p], block),
                ("z", NZ, z, lambda p, h: hb.at[c, x, b_first(p) if h == 0 else b_second(p)], 4 * block),
                ("x", NX, x, lambda p, h: b_piece(c, p, h), 24 * block),
            ],
            b_piece, 24 * block, b_done,
        )
    )
    drive(
        gather(
            "a",
            [
                ("x", NX, x, lambda p, h: ha.at[c, z, y, p, pl.ds(16 * h, 16)], block // 2),
                ("y", NY, y, lambda p, h: ha.at[c, z, p, pl.ds(2 * h, 2)], 2 * block),
                ("z", NZ, z, lambda p, h: a_piece(c, p, h), 8 * block),
            ],
            a_piece, 8 * block, a_done,
        )
    )
    while queue:
        heapq.heappop(queue)[2]()

    slots = itertools.count()

    def combine(tiles):
        peak = functools.reduce(jnp.maximum, [t[0:4] for t in tiles])
        total = sum(t[4:8] * jnp.exp(t[0:4] - peak) for t in tiles)
        return peak, total

    def put(peak, total):
        slot = ls.at[next(slots)]
        slot[0:4] = peak
        slot[4:8] = total
        return slot

    def relay(source, target, device, sends, recvs, index):
        copy = pltpu.make_async_remote_copy(
            src_ref=source, dst_ref=target, send_sem=sends.at[index],
            recv_sem=recvs.at[index], device_id=device, device_id_type=MESH,
        )
        copy.start()
        sent.append(copy)

    own = ls.at[next(slots)]
    for g in range(4):
        tile = acc_out[:, pl.ds(128 * g, 128)]
        peak = jnp.max(tile, axis=0, keepdims=True)
        own[g : g + 1] = peak
        own[4 + g : 5 + g] = jnp.sum(jnp.exp(tile - peak), axis=0, keepdims=True)
    theirs = ls.at[next(slots)]
    index = next(near_count)
    relay(own, theirs, partner, near_send, near_recv, index)
    arrived(theirs, index, near_recv)
    mine = put(*combine([own[...], theirs[...]]))
    for axis, size in (("x", NX), ("y", NY), ("z", NZ)):
        half = size // 2
        steps = [(way, d) for d in range(1, half + 1) for way in (1, -1) if d < half or way > 0]
        where = {step: (ls.at[next(slots)], next(count)) for step in steps}
        for way in (1, -1):
            target, index = where[way, 1]
            relay(mine, target, along(axis, way), send, recv, index)
        for way, d in steps:
            target, index = where[way, d]
            arrived(target, index, recv)
            if (way, d + 1) in where:
                following, index = where[way, d + 1]
                relay(target, following, along(axis, way), send, recv, index)
        peak, total = combine([mine[...]] + [where[step][0][...] for step in steps])
        if axis != "z":
            mine = put(peak, total)
    norm = peak + jnp.log(total)
    for g in range(4):
        norm_out[0:1, pl.ds(128 * g, 128)] = norm[g : g + 1]
    for copy in sent:
        copy.wait_send()


def local(hidden_rows, row_states, head_weight, grammar_table):
    depth, columns = head_weight.shape
    states = grammar_table.shape[0]
    rows = 512
    state_tile = jnp.broadcast_to(jnp.tile(row_states, 4)[None, :], (8, 128))
    anywhere = pl.BlockSpec(memory_space=pl.ANY)
    inside = pl.BlockSpec(memory_space=pltpu.VMEM)
    masked, norm = pl.pallas_call(
        kernel,
        out_shape=(
            jax.ShapeDtypeStruct((columns, rows), jnp.float32),
            jax.ShapeDtypeStruct((1, rows), jnp.float32),
        ),
        in_specs=[anywhere] * 4,
        out_specs=(inside, inside),
        scratch_shapes=[
            pltpu.VMEM((2, NZ, NY, NX, 32, 128), jnp.bfloat16),
            pltpu.VMEM((2, NX, 16, NY, 32, 128), jnp.bfloat16),
            pltpu.VMEM((2, NY, NX, 16, 32, 128), jnp.bfloat16),
            pltpu.VMEM((2, NY, 2, 8, 128), jnp.int32),
            pltpu.VMEM((columns, depth), jnp.bfloat16),
            pltpu.VMEM((columns, states), jnp.int32),
            pltpu.VMEM((24, 8, 128), jnp.float32),
            pltpu.SemaphoreType.DMA((100,)),
            pltpu.SemaphoreType.DMA((100,)),
            pltpu.SemaphoreType.DMA((36,)),
            pltpu.SemaphoreType.DMA((36,)),
            pltpu.SemaphoreType.DMA((8,)),
        ],
        compiler_params=pltpu.CompilerParams(
            collective_id=0, has_side_effects=True, vmem_limit_bytes=56 << 20
        ),
    )(hidden_rows, state_tile, head_weight.T, grammar_table.T)
    log_probs = jnp.where(masked > 0.5 * LOWEST, masked - norm, 0.0)
    return (log_probs.T, norm[0])


def solution(mesh):
    placed = (
        P("vocab", "rows"),
        P("vocab"),
        P(None, ("rows", "vocab")),
        P(None, ("rows", "vocab")),
    )
    return jax.shard_map(
        local,
        mesh=mesh,
        in_specs=placed,
        out_specs=(P(None, ("rows", "vocab")), P()),
        check_vma=False,
    )
```

time: 345 us -> 83.6 us (0.24)
  the two profiles are of different devices: /device:TPU:1 before, /device:TPU:2 now
where the time goes in v2:
time: 83.6 us; the launch traced here: 83.5 us
  Pallas kernels  78.5 us (94%)
  other arithmetic  2.5 us (3%)
  local copies, waits for them, and re-layouts  1.92 us (2%)
    pallas_call x1, Pallas kernels, local(): pl.pallas_call(kernel, out_shape=(jax.ShapeDtypeStruct((columns, rows), j...  78.5 us
    transpose x1, other arithmetic, local(): return (log_probs.T, norm[0])  2.5 us

profile of v2, /device:TPU:2, one launch (start us, length us, event | category | flops | bytes accessed | tf_op | source)
XLA Modules:
  0.0 83.5 jit_solution(11608031514308342681)
XLA Ops:
  0.6 0.7 tile.2
  1.3 0.1 broadcast_in_dim.11
  1.4 0.6 broadcast_in_dim.12.st_in
  2.0 78.5 %shard_map.59 = (f32[594,512]{1,0:T(8,128)}, f32[1,512]{1,0:T(1,128)}) custom-call(bf16[32,512]{1,0:T(8,128)(2,1)} %hid.1, s32[8,128]{1,0:T(8,128)} %broadcast_in_dim.12.st_in, bf16[594,8192]{1,0:T(8,128)(2,1)} %bitcast.5, s32[594,512]{1,0:T(8,128)} %bitcast.6), custom_call_target="tpu_custom_call" | custom-call | tf_op jit(solution)/shard_map/pallas_call | solution.py:412
  80.4 0.0 copy-start
  80.4 2.5 %select_bitcast_fusion = f32[512,594]{0,1:T(8,128)} fusion(f32[594,512]{1,0:T(8,128)} %get-tuple-element.4, f32[512]{0:T(512)} %bitcast.7), kind=kLoop, calls=%fused_computation | loop fusion | flops 912384 | bytes 2435072 | tf_op jit(solution)/shard_map/transpose | solution.py:439
  82.9 0.0 copy-done
  82.9 0.6 copy.7
Async XLA Ops:
  80.4 2.5 %copy-start = (f32[1,512]{1,0:T(1,128)S(1)}, f32[1,512]{1,0:T(1,128)}, u32[]{:S(2)}) copy-start(f32[1,512]{1,0:T(1,128)} %get-tuple-element.5) | copy-start | bytes 6148

commit v3 on v1

v3 whole, which is shorter than its diff:
```python
import heapq
import itertools

import jax
import jax.numpy as jnp
from jax import lax
from jax.experimental import pallas as pl
from jax.experimental.pallas import tpu as pltpu
from jax.sharding import PartitionSpec as P

LOWEST = -1e30
NX, NY, NZ = 4, 4, 8
MESH = pl.DeviceIdType.MESH
NT = (((1,), (1,)), ((), ()))
FIRST_HOP, NEXT_HOP, LINK, NEAR_HOP, NEAR = 2.7, 0.6, 46e3, 1.0, 2e5
A_TASK, G_TASK = 0.4, 0.5


def place(x, y, z, c):
    rows = z * 2 + lax.div(x, 2)
    vocab = lax.rem(x, 2) * 8 + y * 2 + c
    return (rows, vocab)


def shifted(pos, step, size):
    return lax.rem(pos + size + step, size)


def short(step, size):
    return min(step % size, -step % size)


PLANE = sorted(
    [(i, j) for i in range(NX) for j in range(NY) if (i, j) != (0, 0)],
    key=lambda s: -short(s[0], NX) - short(s[1], NY),
)
PLANE_CORES = [(0, 0, 1)] + [(i, j, k) for i, j in PLANE for k in range(2)]
PLANE_CORES = PLANE_CORES[1:] + PLANE_CORES[:1]
COLUMN = sorted(range(1, NZ), key=lambda s: -short(s, NZ))


def kernel(
    hid, st_in, w_in, tab_in, acc_out, norm_out,
    ha, g, st, w, tab, ls, send, recv, near_send, near_recv, bulk_send, bulk_recv, local,
):
    r, v = lax.axis_index("rows"), lax.axis_index("vocab")
    z, x = lax.div(r, 2), lax.rem(r, 2) * 2 + lax.div(v, 8)
    y, c = lax.rem(lax.div(v, 2), NY), lax.rem(v, 2)
    other = 1 - c
    sizes = {"x": NX, "y": NY, "z": NZ}
    here = {"x": x, "y": y, "z": z}

    def away(dx=0, dy=0, dz=0, dc=0):
        return place(
            shifted(x, dx, NX), shifted(y, dy, NY), shifted(z, dz, NZ), c if dc == 0 else other
        )

    x_lo = lax.rem(x, 2)
    q2_slot = jnp.where(lax.rem(z, 2) == 0, 8, 20) + lax.div(z, 2)
    own_slots = (z, q2_slot, 12 + z)

    fills = []

    def fill(source, target):
        copy = pltpu.make_async_copy(source, target, local.at[len(fills)])
        copy.start()
        fills.append(copy)
        return copy

    quarter = [hid.at[:, pl.ds(128 * q, 128)] for q in range(4)]
    for q, slot in zip((1, 2, 3), own_slots):
        fill(quarter[q], g.at[c, x, y, slot])
    fill(quarter[0], ha.at[c, z, y, x])
    fill(st_in, st.at[x_lo, y, c])
    tab_fill = fill(tab_in, tab)
    w_fill = fill(w_in, w)

    barrier = pltpu.get_barrier_semaphore()
    friends = [away(i, j, 0, k) for i, j, k in PLANE_CORES] + [away(dz=s) for s in COLUMN]
    for friend in friends:
        pl.semaphore_signal(barrier, inc=1, device_id=friend, device_id_type=MESH)
    pl.semaphore_wait(barrier, len(friends))
    for copy in fills[:5]:
        copy.wait()

    count, near_count = itertools.count(), itertools.count()
    sent = []

    def remote(source, target, device, send_sem, recv_sem):
        copy = pltpu.make_async_remote_copy(
            src_ref=source, dst_ref=target, send_sem=send_sem, recv_sem=recv_sem,
            device_id=device, device_id_type=MESH,
        )
        copy.start()
        return copy

    def arrived(target, sem):
        pltpu.make_async_copy(target, target, sem).wait()

    clock = [0.0]
    queue = []
    order = itertools.count()
    links = {}

    def post(time, action, rank=0):
        heapq.heappush(queue, (time, rank, next(order), action))

    def through(link, nbytes, rate, latency):
        links[link] = max(clock[0], links.get(link, 0.0)) + nbytes / rate
        return links[link] + latency

    for s in COLUMN:
        for slot in own_slots:
            block = g.at[c, x, y, slot]
            remote(block, block, away(dz=s), bulk_send.at[0], bulk_recv.at[0])
    own_tile = st.at[x_lo, y, c]
    for i, j in PLANE:
        block = ha.at[c, z, y, x]
        remote(block, block, away(i, j), bulk_send.at[1], bulk_recv.at[1])
    x_other = 1 - 2 * x_lo
    for lo in (1, 0):
        for j in range(NY):
            for k in range(2):
                if (lo, j, k) != (0, 0, 0):
                    device = place(
                        x + x_other if lo else x, shifted(y, j, NY), z, c if k == 0 else other
                    )
                    remote(own_tile, own_tile, device, bulk_send.at[2], bulk_recv.at[2])

    done = set()
    near_at = {}
    tasks = []

    def near_landed(unit):
        done.add(unit)
        for task in list(tasks):
            needs, action = task
            if all(n in done for n in needs):
                tasks.remove(task)
                post(clock[0], action, 1)

    def hand_over(unit, piece, nbytes):
        index = next(near_count)
        source = piece(c)
        sent.append(remote(source, source, away(dc=1), near_send.at[index], near_recv.at[index]))
        near_at[unit] = (piece(other), index)
        post(through("near", nbytes, NEAR, NEAR_HOP), lambda: near_landed(unit))

    def take(units):
        for unit in units:
            if unit in near_at:
                target, index = near_at.pop(unit)
                arrived(target, near_recv.at[index])

    def spread(axis, way, d, h, pieces, piece, nbytes, seen):
        size = sizes[axis]
        half = size // 2
        index = next(count)
        source = piece(shifted(here[axis], -way * (d - 1), size), h)
        device = away(**{"d" + axis: way})
        sent.append(remote(source, source, device, send.at[index], recv.at[index]))

        def land():
            origin = shifted(here[axis], -way * d, size)
            arrived(piece(origin, h), recv.at[index])
            final = h < pieces // 2 if way > 0 else h >= pieces // 2
            if d + 1 < half or (d + 1 == half and final):
                spread(axis, way, d + 1, h, pieces, piece, nbytes, seen)
            seen(-way * d if d < half else half, origin, h)

        post(through((axis, way), nbytes, LINK, FIRST_HOP), land)

    def around(axis, pieces, piece, nbytes, seen):
        for i in range(pieces):
            spread(axis, 1, 1, i, pieces, piece, nbytes, seen)
            spread(axis, -1, 1, pieces - 1 - i, pieces, piece, nbytes, seen)

    block_bytes = 32 * 128 * 2
    unit_bytes = 6 * block_bytes

    def unit_piece(xx, yy, k):
        return lambda core: g.at[core, xx, yy, pl.ds(6 * k, 6)]

    def column_ready():
        arrived(g.at[c, x, y, pl.ds(0, 21)], bulk_recv.at[0])

        def colour(first, last, ks):
            def at(p_first, p_last, k):
                where = {first: p_first, last: p_last}
                return unit_piece(where["x"], where["y"], k)

            def onward(rel_first, p_first, h):
                k = ks[h]

                def seen(rel_last, p_last, _):
                    rel = {first: rel_first, last: rel_last}
                    hand_over((rel["x"], rel["y"], k), at(p_first, p_last, k), unit_bytes)

                for way in (1, -1):
                    spread(
                        last, way, 1, h, 2, lambda p, hh: at(p_first, p, ks[hh])(c), unit_bytes, seen
                    )

            def seen_first(rel_first, p_first, h):
                onward(rel_first, p_first, h)
                rel = {first: rel_first, last: 0}
                hand_over((rel["x"], rel["y"], ks[h]), at(p_first, here[last], ks[h]), unit_bytes)

            return (
                lambda: around(
                    first, 2, lambda p, h: at(p, here[last], ks[h])(c), unit_bytes, seen_first
                ),
                lambda: [onward(0, here[first], h) for h in range(2)],
            )

        b_first, b_last = colour("y", "x", (0, 1))
        c_first, c_last = colour("x", "y", (2, 3))
        b_first()
        c_first()
        b_last()
        c_last()
        for k in range(4):
            hand_over((0, 0, k), unit_piece(x, y, k), unit_bytes)

    def plane_ready():
        arrived(g.at[c, x, y, pl.ds(0, 15)], bulk_recv.at[1])
        piece = lambda core, p, h: ha.at[core, p, h]

        def seen(rel, p, h):
            hand_over(("a", rel, h), lambda core: piece(core, p, h), 4 * block_bytes)

        around("z", 4, lambda p, h: piece(c, p, h), 4 * block_bytes, seen)
        hand_over(("a", 0, 0), lambda core: ha.at[core, z], 16 * block_bytes)

    def weights(offsets):
        return jnp.concatenate(
            [w[:, pl.ds(pl.multiple_of(o, 128), 128)] for o in offsets], axis=1
        )

    def stack(parts):
        return jnp.concatenate(parts, axis=0)

    def a_task(zz):
        rhs = jnp.concatenate(
            [
                stack(
                    [
                        ha[core, zz, yy, 2 * hi + lo]
                        for lo in range(2) for yy in range(NY) for core in range(2)
                    ]
                )
                for hi in range(2)
            ],
            axis=1,
        )
        lhs = weights([(2 * zz + hi) * 512 for hi in range(2)])
        acc_out[...] += lax.dot_general(lhs, rhs, NT, preferred_element_type=jnp.float32)

    def column_of(slot, hi):
        if slot < 8:
            return (2 * slot + hi) * 512 + 128
        if slot < 12:
            return (4 * (slot - 8) + hi) * 512 + 256
        if slot < 20:
            return (2 * (slot - 12) + hi) * 512 + 384
        return (4 * (slot - 20) + 2 + hi) * 512 + 256

    def b_task(xx, k):
        hi, lo = lax.div(xx, 2), lax.rem(xx, 2)
        slots = range(6 * k, 6 * k + 6)
        rhs = jnp.concatenate(
            [stack([g[core, xx, yy, s] for yy in range(NY) for core in range(2)]) for s in slots],
            axis=1,
        )
        lanes = pl.ds(pl.multiple_of(lo * 256, 128), 256)
        acc_out[:, lanes] += lax.dot_general(
            weights([column_of(s, hi) for s in slots]), rhs, NT, preferred_element_type=jnp.float32
        )

    def c_task(hi, pair, k):
        slots = range(6 * k, 6 * k + 6)
        rhs = jnp.concatenate(
            [
                stack(
                    [
                        g[core, 2 * hi + lo, 2 * pair + yy, s]
                        for lo in range(2) for yy in range(2) for core in range(2)
                    ]
                )
                for s in slots
            ],
            axis=1,
        )
        out = lax.dot_general(
            weights([column_of(s, hi) for s in slots]), rhs, NT, preferred_element_type=jnp.float32
        )
        for lo in range(2):
            lanes = pl.ds(pl.multiple_of(lo * 256 + pair * 128, 128), 128)
            acc_out[:, lanes] += out[:, lo * 128 : (lo + 1) * 128]

    def add_task(needs, cost, work):
        def action():
            take(needs)
            work()
            clock[0] += cost

        tasks.append((needs, action))

    for rel in (0, 1, -1, 2, -2, 3, -3, 4):
        needs = [("a", rel, h) for h in range(4)] if rel else [("a", 0, 0)]
        add_task(
            ["start"] + needs, A_TASK, lambda rel=rel: a_task(shifted(z, rel, NZ))
        )
    for rel in (0, 1, -1, 2):
        for k in (0, 1):
            add_task(
                ["start"] + [(rel, dy, k) for dy in (0, 1, -1, 2)], G_TASK,
                lambda rel=rel, k=k: b_task(shifted(x, rel, NX), k),
            )
    close, far = (0, 1, -1), (1, -1, 2)
    for dxs in (close, far):
        for dys in (close, far):
            for k in (2, 3):
                add_task(
                    ["start"] + [(dx, dy, k) for dx in dxs for dy in dys], G_TASK,
                    lambda dxs=dxs, dys=dys, k=k: c_task(
                        lax.div(x, 2) if dxs is close else 1 - lax.div(x, 2),
                        lax.div(y, 2) if dys is close else 1 - lax.div(y, 2),
                        k,
                    ),
                )

    def begin():
        arrived(ls.at[pl.ds(1, 15)], bulk_recv.at[2])
        tab_fill.wait()
        group = lax.div(lax.broadcasted_iota(jnp.int32, (1, 128), 1), 32)
        parts = []
        for lo in range(2):
            for pair in range(2):
                picked = st[lo, 2 * pair + 1, 1, 0:1]
                for k in range(3):
                    picked = jnp.where(group == k, st[lo, 2 * pair + k // 2, k % 2, 0:1], picked)
                parts.append(picked)
        row_states = jnp.concatenate(parts, axis=1)
        marks = lax.broadcasted_iota(jnp.int32, (tab.shape[1], row_states.shape[1]), 0)
        onehot = jnp.where(marks == row_states, 1.0, 0.0).astype(jnp.bfloat16)
        allowed = jnp.dot(
            tab[...].astype(jnp.float32).astype(jnp.bfloat16), onehot, preferred_element_type=jnp.float32
        )
        acc_out[...] = jnp.where(allowed > 0.5, 0.0, LOWEST)
        w_fill.wait()
        clock[0] += 1.0
        near_landed("start")

    post(6.0, plane_ready)
    post(7.0, column_ready)
    post(7.5, begin)
    while queue:
        time, _, _, action = heapq.heappop(queue)
        clock[0] = max(clock[0], time)
        action()

    own = ls.at[0]
    for k in range(4):
        tile = acc_out[:, pl.ds(128 * k, 128)]
        peak = jnp.max(tile, axis=0, keepdims=True)
        own[k : k + 1] = peak
        own[4 + k : 5 + k] = jnp.sum(jnp.exp(tile - peak), axis=0, keepdims=True)

    def combine(first, number):
        peaks, totals = ls[first : first + number, 0:4], ls[first : first + number, 4:8]
        peak = jnp.max(peaks, axis=0)
        return peak, jnp.sum(totals * jnp.exp(peaks - peak[None]), axis=0)

    for n, (i, j, k) in enumerate(PLANE_CORES):
        remote(own, ls.at[1 + n], away(i, j, 0, k), bulk_send.at[3], bulk_recv.at[3])
    arrived(ls.at[pl.ds(1, 31)], bulk_recv.at[3])
    mine = ls.at[32]
    mine[0:4], mine[4:8] = combine(0, 32)
    for n, s in enumerate(COLUMN):
        remote(mine, ls.at[33 + n], away(dz=s), bulk_send.at[4], bulk_recv.at[4])
    arrived(ls.at[pl.ds(33, 7)], bulk_recv.at[4])
    peak, total = combine(32, 8)
    norm = peak + jnp.log(total)
    for k in range(4):
        norm_out[0:1, pl.ds(128 * k, 128)] = norm[k : k + 1]

    for copy in sent:
        copy.wait_send()
    arrived(g.at[c, x, y, pl.ds(0, 21)], bulk_send.at[0])
    arrived(g.at[c, x, y, pl.ds(0, 15)], bulk_send.at[1])
    arrived(ls.at[pl.ds(1, 15)], bulk_send.at[2])
    arrived(ls.at[pl.ds(1, 31)], bulk_send.at[3])
    arrived(ls.at[pl.ds(33, 7)], bulk_send.at[4])


def local(hidden_rows, row_states, head_weight, grammar_table):
    depth, columns = head_weight.shape
    states = grammar_table.shape[0]
    rows = 512
    state_tile = jnp.broadcast_to(jnp.tile(row_states, 4)[None, :], (8, 128))
    anywhere = pl.BlockSpec(memory_space=pl.ANY)
    inside = pl.BlockSpec(memory_space=pltpu.VMEM)
    masked, norm = pl.pallas_call(
        kernel,
        out_shape=(
            jax.ShapeDtypeStruct((columns, rows), jnp.float32),
            jax.ShapeDtypeStruct((1, rows), jnp.float32),
        ),
        in_specs=[anywhere] * 4,
        out_specs=(inside, inside),
        scratch_shapes=[
            pltpu.VMEM((2, NZ, NY, NX, 32, 128), jnp.bfloat16),
            pltpu.VMEM((2, NX, NY, 24, 32, 128), jnp.bfloat16),
            pltpu.VMEM((2, NY, 2, 8, 128), jnp.int32),
            pltpu.VMEM((columns, depth), jnp.bfloat16),
            pltpu.VMEM((columns, states), jnp.int32),
            pltpu.VMEM((40, 8, 128), jnp.float32),
            pltpu.SemaphoreType.DMA((92,)),
            pltpu.SemaphoreType.DMA((92,)),
            pltpu.SemaphoreType.DMA((96,)),
            pltpu.SemaphoreType.DMA((96,)),
            pltpu.SemaphoreType.DMA((5,)),
            pltpu.SemaphoreType.DMA((5,)),
            pltpu.SemaphoreType.DMA((8,)),
        ],
        compiler_params=pltpu.CompilerParams(
            collective_id=0, has_side_effects=True, vmem_limit_bytes=56 << 20
        ),
    )(hidden_rows, state_tile, head_weight.T, grammar_table.T)
    log_probs = jnp.where(masked > 0.5 * LOWEST, masked - norm, 0.0)
    return (log_probs.T, norm[0])


def solution(mesh):
    placed = (
        P("vocab", "rows"),
        P("vocab"),
        P(None, ("rows", "vocab")),
        P(None, ("rows", "vocab")),
    )
    return jax.shard_map(
        local,
        mesh=mesh,
        in_specs=placed,
        out_specs=(P(None, ("rows", "vocab")), P()),
        check_vma=False,
    )
```

time: 345 us -> 63.3 us (0.18)
  blocking collectives: 181 us -> 0 us
  waiting for transfers between devices: 133 us -> 0 us
  Pallas kernels: 0 us -> 58.1 us
  between operations: 14.7 us -> 0.65 us
  matrix products: 12.4 us -> 0 us
    all_gather x1 -> x0, waiting for transfers between devices: 133 us -> none  [local(): every = lax.all_gather(block, 'rows', axis=1, tiled=True)]
    pmax x1 -> x0, blocking collectives: 78.6 us -> none  [local(): row_peak = lax.pmax(own_peak, ('rows', 'vocab'))]
    psum x1 -> x0, blocking collectives: 72.4 us -> none  [local(): lax.psum(own_total * jnp.exp(own_peak - row_peak), ('rows', 'vocab'))]
    pallas_call x0 -> x1, Pallas kernels: none -> 58.1 us  [local(): pl.pallas_call(kernel, out_shape=(jax.ShapeDtypeStruct((columns, rows), j...]
    all_gather x1 -> x0, blocking collectives: 24.3 us -> none  [local(): block = lax.all_gather(hidden_rows, 'vocab', axis=0, tiled=True)]
    dot_general x2 -> x0, matrix products: 12.4 us -> none  [the longest x1 10.5 us: local(): lax.dot_general(head_weight, every, (((0,), (1,)), ((), ())), preferred_e...]
    unnamed x1 -> x0, blocking collectives: 5.89 us -> none
  transfers between devices with their start and end apart: 1 -> 0, of which waited for: 1 -> 0; matrix products, arithmetic and copies ran while one was open for 1% -> 0% of each run, Pallas kernels for 0% -> 0%
where the time goes in v3:
time: 63.3 us; the launch traced here: 63.2 us
  Pallas kernels  58.1 us (92%)
  other arithmetic  2.5 us (4%)
  local copies, waits for them, and re-layouts  1.92 us (3%)
  between operations  0.65 us (1%)
    pallas_call x1, Pallas kernels, local(): pl.pallas_call(kernel, out_shape=(jax.ShapeDtypeStruct((columns, rows), j...  58.1 us
    transpose x1, other arithmetic, local(): return (log_probs.T, norm[0])  2.5 us

profile of v3, /device:TPU:1, one launch (start us, length us, event | category | flops | bytes accessed | tf_op | source)
XLA Modules:
  0.0 63.2 jit_solution(6164077196303820603)
XLA Ops:
  0.6 0.7 %tile.2 = s32[4,32]{1,0:T(4,128)S(1)} broadcast(s32[32]{0:T(128)} %param.5), dimensions={1} | broadcast | bytes 640 | tf_op jit(solution)/shard_map/tile | solution.py:401
  1.3 0.1 broadcast_in_dim.11
  1.4 0.6 broadcast_in_dim.12.st_in
  2.0 58.1 %shard_map.59 = (f32[594,512]{1,0:T(8,128)}, f32[1,512]{1,0:T(1,128)}) custom-call(bf16[32,512]{1,0:T(8,128)(2,1)} %hid.1, s32[8,128]{1,0:T(8,128)} %broadcast_in_dim.12.st_in, bf16[594,8192]{1,0:T(8,128)(2,1)} %bitcast.5, s32[594,512]{1,0:T(8,128)} %bitcast.6), custom_call_target="tpu_custom_call" | custom-call | tf_op jit(solution)/shard_map/pallas_call | solution.py:404
  60.1 0.0 copy-start
  60.1 2.5 %select_bitcast_fusion = f32[512,594]{0,1:T(8,128)} fusion(f32[594,512]{1,0:T(8,128)} %get-tuple-element.4, f32[512]{0:T(512)} %bitcast.7), kind=kLoop, calls=%fused_computation | loop fusion | flops 912384 | bytes 2435072 | tf_op jit(solution)/shard_map/transpose | solution.py:432
  62.6 0.0 copy-done
  62.6 0.6 copy.7
Async XLA Ops:
  60.1 2.5 %copy-start = (f32[1,512]{1,0:T(1,128)S(1)}, f32[1,512]{1,0:T(1,128)}, u32[]{:S(2)}) copy-start(f32[1,512]{1,0:T(1,128)} %get-tuple-element.5) | copy-start | bytes 6148

commit v4 on v3

--- a/solution.py
+++ b/solution.py
@@ -12,8 +12,8 @@
 NX, NY, NZ = 4, 4, 8
 MESH = pl.DeviceIdType.MESH
 NT = (((1,), (1,)), ((), ()))
-FIRST_HOP, NEXT_HOP, LINK, NEAR_HOP, NEAR = 2.7, 0.6, 46e3, 1.0, 2e5
-A_TASK, G_TASK = 0.4, 0.5
+FIRST_HOP, NEXT_HOP, LINK, NEAR_HOP, NEAR = 2.3, 0.6, 90e3, 1.0, 6e5
+A_TASK, G_TASK = 0.2, 0.4
 
 
 def place(x, y, z, c):
@@ -41,7 +41,7 @@
 
 def kernel(
     hid, st_in, w_in, tab_in, acc_out, norm_out,
-    ha, g, st, w, tab, ls, send, recv, near_send, near_recv, bulk_send, bulk_recv, local,
+    ha, g, st, raw, w, tab, ls, send, recv, near_send, near_recv, bulk_send, bulk_recv, local,
 ):
     r, v = lax.axis_index("rows"), lax.axis_index("vocab")
     z, x = lax.div(r, 2), lax.rem(r, 2) * 2 + lax.div(v, 8)
@@ -71,7 +71,7 @@
     for q, slot in zip((1, 2, 3), own_slots):
         fill(quarter[q], g.at[c, x, y, slot])
     fill(quarter[0], ha.at[c, z, y, x])
-    fill(st_in, st.at[x_lo, y, c])
+    fill(st_in, raw)
     tab_fill = fill(tab_in, tab)
     w_fill = fill(w_in, w)
 
@@ -82,6 +82,7 @@
     pl.semaphore_wait(barrier, len(friends))
     for copy in fills[:5]:
         copy.wait()
+    st[x_lo, y, c] = jnp.broadcast_to(jnp.concatenate([raw[...]] * 4, axis=1), (8, 128))
 
     count, near_count = itertools.count(), itertools.count()
     sent = []
@@ -198,7 +199,7 @@
 
                 for way in (1, -1):
                     spread(
-                        last, way, 1, h, 2, lambda p, hh: at(p_first, p, ks[hh])(c), unit_bytes, seen
+                        last, way, 1, h, 2, lambda p, hh: at(p_first, p, ks[hh])(c), unit_bytes, seen,
                     )
 
             def seen_first(rel_first, p_first, h):
@@ -224,12 +225,12 @@
 
     def plane_ready():
         arrived(g.at[c, x, y, pl.ds(0, 15)], bulk_recv.at[1])
-        piece = lambda core, p, h: ha.at[core, p, h]
+        piece = lambda core, p, h: ha.at[core, p, pl.ds(2 * h, 2)]
 
         def seen(rel, p, h):
-            hand_over(("a", rel, h), lambda core: piece(core, p, h), 4 * block_bytes)
-
-        around("z", 4, lambda p, h: piece(c, p, h), 4 * block_bytes, seen)
+            hand_over(("a", rel, h), lambda core: piece(core, p, h), 8 * block_bytes)
+
+        around("z", 2, lambda p, h: piece(c, p, h), 8 * block_bytes, seen)
         hand_over(("a", 0, 0), lambda core: ha.at[core, z], 16 * block_bytes)
 
     def weights(offsets):
@@ -307,7 +308,7 @@
         tasks.append((needs, action))
 
     for rel in (0, 1, -1, 2, -2, 3, -3, 4):
-        needs = [("a", rel, h) for h in range(4)] if rel else [("a", 0, 0)]
+        needs = [("a", rel, h) for h in range(2)] if rel else [("a", 0, 0)]
         add_task(
             ["start"] + needs, A_TASK, lambda rel=rel: a_task(shifted(z, rel, NZ))
         )
@@ -354,7 +355,7 @@
 
     post(6.0, plane_ready)
     post(7.0, column_ready)
-    post(7.5, begin)
+    post(6.5, begin)
     while queue:
         time, _, _, action = heapq.heappop(queue)
         clock[0] = max(clock[0], time)
@@ -398,7 +399,7 @@
     depth, columns = head_weight.shape
     states = grammar_table.shape[0]
     rows = 512
-    state_tile = jnp.broadcast_to(jnp.tile(row_states, 4)[None, :], (8, 128))
+    operands = (hidden_rows, row_states[None, :], head_weight.T, grammar_table.T)
     anywhere = pl.BlockSpec(memory_space=pl.ANY)
     inside = pl.BlockSpec(memory_space=pltpu.VMEM)
     masked, norm = pl.pallas_call(
@@ -413,6 +414,7 @@
             pltpu.VMEM((2, NZ, NY, NX, 32, 128), jnp.bfloat16),
             pltpu.VMEM((2, NX, NY, 24, 32, 128), jnp.bfloat16),
             pltpu.VMEM((2, NY, 2, 8, 128), jnp.int32),
+            pltpu.VMEM((1, 32), jnp.int32),
             pltpu.VMEM((columns, depth), jnp.bfloat16),
             pltpu.VMEM((columns, states), jnp.int32),
             pltpu.VMEM((40, 8, 128), jnp.float32),
@@ -425,9 +427,9 @@
             pltpu.SemaphoreType.DMA((8,)),
         ],
         compiler_params=pltpu.CompilerParams(
-            collective_id=0, has_side_effects=True, vmem_limit_bytes=56 << 20
+            collective_id=0, has_side_effects=True, vmem_limit_bytes=40 << 20
         ),
-    )(hidden_rows, state_tile, head_weight.T, grammar_table.T)
+    )(*(pltpu.with_memory_space_constraint(a, pltpu.HBM) for a in operands))
     log_probs = jnp.where(masked > 0.5 * LOWEST, masked - norm, 0.0)
     return (log_probs.T, norm[0])
 

time: 63.3 us -> 57.7 us (0.912)
  Pallas kernels: 58.1 us -> 55.1 us
  local copies, waits for them, and re-layouts: 1.92 us -> 0.58 us
  other arithmetic: 2.5 us -> 1.21 us
    pallas_call x1, Pallas kernels: 58.1 us -> 55.1 us  [local(): pl.pallas_call(kernel, out_shape=(jax.ShapeDtypeStruct((columns, rows), j...]
    transpose x1, other arithmetic: 2.5 us -> 1.21 us  [local(): return (log_probs.T, norm[0])]
    broadcast_in_dim x2 -> x0, local copies, waits for them, and re-layouts: 0.68 us -> none  [local(): state_tile = jnp.broadcast_to(jnp.tile(row_states, 4)[None, :], (8, 128))]
    another operation x1 -> x0, local copies, waits for them, and re-layouts: 0.66 us -> none  [local(): state_tile = jnp.broadcast_to(jnp.tile(row_states, 4)[None, :], (8, 128))]
where the time goes in v4:
time: 57.7 us; the launch traced here: 57.6 us
  Pallas kernels  55.1 us (95%)
  other arithmetic  1.21 us (2%)
  between operations  0.64 us (1%)
  local copies, waits for them, and re-layouts  0.58 us (1%)
    pallas_call x1, Pallas kernels, local(): pl.pallas_call(kernel, out_shape=(jax.ShapeDtypeStruct((columns, rows), j...  55.1 us
    transpose x1, other arithmetic, local(): return (log_probs.T, norm[0])  1.21 us

profile of v4, /device:TPU:1, one launch (start us, length us, event | category | flops | bytes accessed | tf_op | source)
XLA Modules:
  0.0 57.6 jit_solution(2634901237481261423)
XLA Ops:
  0.6 55.1 %shard_map.59 = (f32[594,512]{1,0:T(8,128)S(1)}, f32[1,512]{1,0:T(1,128)S(1)}) custom-call(bf16[32,512]{1,0:T(8,128)(2,1)} %hid.1, s32[1,32]{1,0:T(1,128)} %bitcast.10, bf16[594,8192]{1,0:T(8,128)(2,1)} %bitcast.8, s32[594,512]{1,0:T(8,128)} %bitcast.9), custom_call_target="tpu_custom_call" | custom-call | tf_op jit(solution)/shard_map/pallas_call | solution.py:405
  55.8 1.2 %select_bitcast_fusion = f32[512,594]{0,1:T(8,128)} fusion(f32[594,512]{1,0:T(8,128)S(1)} %get-tuple-element.4, f32[512]{0:T(512)S(1)} %bitcast.6), kind=kLoop, calls=%fused_computation | loop fusion | flops 912384 | bytes 2435072 | tf_op jit(solution)/shard_map/transpose | solution.py:434
  57.0 0.6 %copy.7 = f32[512]{0:T(512)} copy(f32[512]{0:T(512)S(1)} %bitcast.7) | data formatting | bytes 4096

commit v5 on v4

--- a/solution.py
+++ b/solution.py
@@ -332,7 +332,7 @@
                 )
 
     def begin():
-        arrived(ls.at[pl.ds(1, 15)], bulk_recv.at[2])
+        arrived(ls.at[pl.ds(1, 30)], bulk_recv.at[2])
         tab_fill.wait()
         group = lax.div(lax.broadcasted_iota(jnp.int32, (1, 128), 1), 32)
         parts = []
@@ -365,24 +365,22 @@
     for k in range(4):
         tile = acc_out[:, pl.ds(128 * k, 128)]
         peak = jnp.max(tile, axis=0, keepdims=True)
-        own[k : k + 1] = peak
-        own[4 + k : 5 + k] = jnp.sum(jnp.exp(tile - peak), axis=0, keepdims=True)
+        own[k : k + 1] = peak + jnp.log(jnp.sum(jnp.exp(tile - peak), axis=0, keepdims=True))
 
     def combine(first, number):
-        peaks, totals = ls[first : first + number, 0:4], ls[first : first + number, 4:8]
-        peak = jnp.max(peaks, axis=0)
-        return peak, jnp.sum(totals * jnp.exp(peaks - peak[None]), axis=0)
+        values = ls[first : first + number]
+        peak = jnp.max(values, axis=0)
+        return peak + jnp.log(jnp.sum(jnp.exp(values - peak[None]), axis=0))
 
     for n, (i, j, k) in enumerate(PLANE_CORES):
         remote(own, ls.at[1 + n], away(i, j, 0, k), bulk_send.at[3], bulk_recv.at[3])
     arrived(ls.at[pl.ds(1, 31)], bulk_recv.at[3])
     mine = ls.at[32]
-    mine[0:4], mine[4:8] = combine(0, 32)
+    mine[...] = combine(0, 32)
     for n, s in enumerate(COLUMN):
         remote(mine, ls.at[33 + n], away(dz=s), bulk_send.at[4], bulk_recv.at[4])
     arrived(ls.at[pl.ds(33, 7)], bulk_recv.at[4])
-    peak, total = combine(32, 8)
-    norm = peak + jnp.log(total)
+    norm = combine(32, 8)
     for k in range(4):
         norm_out[0:1, pl.ds(128 * k, 128)] = norm[k : k + 1]
 
@@ -390,7 +388,7 @@
         copy.wait_send()
     arrived(g.at[c, x, y, pl.ds(0, 21)], bulk_send.at[0])
     arrived(g.at[c, x, y, pl.ds(0, 15)], bulk_send.at[1])
-    arrived(ls.at[pl.ds(1, 15)], bulk_send.at[2])
+    arrived(ls.at[pl.ds(1, 30)], bulk_send.at[2])
     arrived(ls.at[pl.ds(1, 31)], bulk_send.at[3])
     arrived(ls.at[pl.ds(33, 7)], bulk_send.at[4])
 
@@ -417,7 +415,7 @@
             pltpu.VMEM((1, 32), jnp.int32),
             pltpu.VMEM((columns, depth), jnp.bfloat16),
             pltpu.VMEM((columns, states), jnp.int32),
-            pltpu.VMEM((40, 8, 128), jnp.float32),
+            pltpu.VMEM((40, 4, 128), jnp.float32),
             pltpu.SemaphoreType.DMA((92,)),
             pltpu.SemaphoreType.DMA((92,)),
             pltpu.SemaphoreType.DMA((96,)),

time: 57.7 us -> 57.6 us (level)
  no operation moved by 1% of the time
where the time goes in v5:
time: 57.6 us; the launch traced here: 57.5 us
  Pallas kernels  55.1 us (96%)
  other arithmetic  1.21 us (2%)
  between operations  0.64 us (1%)
  local copies, waits for them, and re-layouts  0.58 us (1%)
    pallas_call x1, Pallas kernels, local(): pl.pallas_call(kernel, out_shape=(jax.ShapeDtypeStruct((columns, rows), j...  55.1 us
    transpose x1, other arithmetic, local(): return (log_probs.T, norm[0])  1.21 us

profile of v5, /device:TPU:1, one launch (start us, length us, event | category | flops | bytes accessed | tf_op | source)
XLA Modules:
  0.0 57.5 jit_solution(12541283931947150086)
XLA Ops:
  0.6 55.1 %shard_map.59 = (f32[594,512]{1,0:T(8,128)S(1)}, f32[1,512]{1,0:T(1,128)S(1)}) custom-call(bf16[32,512]{1,0:T(8,128)(2,1)} %hid.1, s32[1,32]{1,0:T(1,128)} %bitcast.10, bf16[594,8192]{1,0:T(8,128)(2,1)} %bitcast.8, s32[594,512]{1,0:T(8,128)} %bitcast.9), custom_call_target="tpu_custom_call" | custom-call | tf_op jit(solution)/shard_map/pallas_call | solution.py:403
  55.7 1.2 %select_bitcast_fusion = f32[512,594]{0,1:T(8,128)} fusion(f32[594,512]{1,0:T(8,128)S(1)} %get-tuple-element.4, f32[512]{0:T(512)S(1)} %bitcast.6), kind=kLoop, calls=%fused_computation | loop fusion | flops 912384 | bytes 2435072 | tf_op jit(solution)/shard_map/transpose | solution.py:432
  57.0 0.6 %copy.7 = f32[512]{0:T(512)} copy(f32[512]{0:T(512)S(1)} %bitcast.7) | data formatting | bytes 4096
